TPU v7x, 256 devices: a whole 4x4x8 slice. The times are simulated.
256 devices in a mesh: file: 8 (over x, core), blk: 32 (over z, y).
Axes of the slice: x: 4, y: 4, z: 8, core: 2. Of those that a mesh axis runs over, the one named last changes fastest.
Arguments:
- ctx_keys: bfloat16 [32768, 256], P(('file', 'blk')), parts along dimension 0, may hold values from -4 to 4
- ctx_values: bfloat16 [32768, 256], P(('file', 'blk')), parts along dimension 0, may hold values from -6 to 6
- middle_queries: bfloat16 [32768, 1792], P(('file', 'blk')), parts along dimension 0, may hold values from -40 to 40
- span_keys: bfloat16 [32768, 256], P(('file', 'blk')), parts along dimension 0, may hold values from -6 to 6
- span_values: bfloat16 [32768, 256], P(('file', 'blk')), parts along dimension 0, may hold values from -6 to 6
- span_len: int32 [256], P(('file', 'blk')), parts along dimension 0, may hold values from 36 to 128, as said below
- commit_pos: int32 [256, 2, 16], P(('file', 'blk')), parts along dimension 0, may hold values from 4 to 127, as said below
- commit_emb: bfloat16 [256, 2, 16, 3584], P(('file', 'blk')), parts along dimension 0, may hold values from -6 to 6
- w_key: bfloat16 [3584, 256], replicated, may hold values from -0.09375 to 0.09375
- w_value: bfloat16 [3584, 256], replicated, may hold values from -0.09375 to 0.09375
Outputs:
- span_out: bfloat16 [2, 32768, 1792], P(None, ('file', 'blk')), parts along dimension 1
There are 8 independent parts, one for each index of `file`. A program takes and returns all parts, laid end to end along the dimension named above; an argument that names none is the same for every part. Nothing has to cross between parts.
Inputs may be any that keep to these rules, and one draw needn't show every extreme that they name: `span_len`: some device's span fills all 128 slots in every draw. `commit_pos`: each device commits exactly 16 slots a step; a device's committed slots are distinct over all steps and lie below that device's span length.
All inputs are finite; a program needn't handle non-finite values.
Results may differ from a plain program's by a relative error of at most 0.0067.
Values may be sent and summed in bfloat16 or wider, within the bound.
No kernel may reach another device: no remote copies, remote signals or barrier semaphores. Data moves between devices by JAX's collectives and lax.ppermute only.
A program may use at most 256 MiB of HBM per device.

v0:
```python
import math
import jax
import jax.numpy as jnp
from jax import lax
from jax.sharding import PartitionSpec as P

HEAD_WIDTH = 128
KEY_VALUE_HEADS = 2
STEPS = 2
QUERY_PER_KEY = 7


def attend_piece(carried, heads_of_queries, key_matrix, value_matrix, live_keys):
    row_max, row_sum, weighted = carried
    row_count = key_matrix.shape[0]
    heads_of_keys = key_matrix.reshape(row_count, KEY_VALUE_HEADS, HEAD_WIDTH)
    heads_of_values = value_matrix.reshape(row_count, KEY_VALUE_HEADS, HEAD_WIDTH)
    scores = jnp.einsum(
        "sgrd,kgd->gsrk", heads_of_queries, heads_of_keys, preferred_element_type=jnp.float32
    ) / math.sqrt(HEAD_WIDTH)
    scores = jnp.where(live_keys[None, None, None, :], scores, -jnp.inf)
    new_max = jnp.maximum(row_max, jnp.max(scores, axis=-1))
    expw = jnp.exp(scores - new_max[..., None])
    row_sum = jnp.sum(expw, axis=-1)
    weighted = jnp.einsum(
        "gsrk,kgd->gsrd",
        expw.astype(jnp.bfloat16),
        heads_of_values,
        preferred_element_type=jnp.float32,
    )
    return (new_max, row_sum, weighted)


def per_device(
    ctx_keys,
    ctx_values,
    middle_queries,
    span_keys,
    span_values,
    span_len,
    commit_pos,
    commit_emb,
    w_key,
    w_value,
):
    local_rows = middle_queries.shape[0]
    slots = jnp.arange(local_rows, dtype=jnp.int32)
    live_here = slots < span_len[0]
    span_flags = live_here.astype(jnp.bfloat16)
    heads_of_queries = middle_queries.reshape(
        local_rows, KEY_VALUE_HEADS, QUERY_PER_KEY, HEAD_WIDTH
    )
    starting = (
        jnp.full((KEY_VALUE_HEADS, local_rows, QUERY_PER_KEY), -1e30, jnp.float32),
        jnp.zeros((KEY_VALUE_HEADS, local_rows, QUERY_PER_KEY), jnp.float32),
        jnp.zeros((KEY_VALUE_HEADS, local_rows, QUERY_PER_KEY, HEAD_WIDTH), jnp.float32),
    )
    keys_now = span_keys
    values_now = span_values
    committed = jnp.zeros((local_rows,), bool)
    attention_outputs = []
    for number in range(STEPS):
        embedded = commit_emb[0, number]
        new_keys = jnp.dot(embedded, w_key, preferred_element_type=jnp.float32).astype(jnp.bfloat16)
        new_values = jnp.dot(embedded, w_value, preferred_element_type=jnp.float32).astype(
            jnp.bfloat16
        )
        slot_ids = commit_pos[0, number]
        committed = committed | jnp.any(slots[:, None] == slot_ids[None, :], axis=1)
        active = live_here & ~committed
        keys_now = keys_now.at[slot_ids].set(new_keys)
        values_now = values_now.at[slot_ids].set(new_values)
        joined_keys = jnp.concatenate([ctx_keys, keys_now])
        joined_values = jnp.concatenate([ctx_values, values_now])
        joined_flags = jnp.concatenate([jnp.ones((ctx_keys.shape[0],), jnp.bfloat16), span_flags])
        row_max, row_sum, weighted = attend_piece(
            starting,
            heads_of_queries,
            lax.all_gather(joined_keys, "blk", axis=0, tiled=True),
            lax.all_gather(joined_values, "blk", axis=0, tiled=True),
            lax.all_gather(joined_flags, "blk", axis=0, tiled=True) > 0.5,
        )
        attention_output = (
            (weighted / row_sum[..., None])
            .transpose(1, 0, 2, 3)
            .reshape(local_rows, KEY_VALUE_HEADS * QUERY_PER_KEY * HEAD_WIDTH)
        )
        attention_outputs.append(
            jnp.where(active[:, None], attention_output, 0.0).astype(jnp.bfloat16)
        )
    return jnp.stack(attention_outputs)


def solution(mesh):
    in_specs = (
        P(("file", "blk"), None),
        P(("file", "blk"), None),
        P(("file", "blk"), None),
        P(("file", "blk"), None),
        P(("file", "blk"), None),
        P(("file", "blk")),
        P(("file", "blk"), None, None),
        P(("file", "blk"), None, None, None),
        P(),
        P(),
    )
    out_specs = P(None, ("file", "blk"), None)
    return jax.shard_map(
        per_device, mesh=mesh, in_specs=in_specs, out_specs=out_specs, check_vma=False
    )
```

profile of v0, /device:TPU:2, one launch (start us, length us, event | category | flops | bytes accessed | tf_op | source)
XLA Modules:
  0.0 381.8 jit_solution(502001056477325090)
XLA Ops:
  6.5 0.0 copy-start
  6.5 0.0 all-gather.6.cloned.1.call-start
  6.5 1.0 copy.77
  7.5 0.8 copy.78
  8.4 0.0 copy-done
  8.4 1.2 convolution_convert_fusion.3
  9.6 1.3 convolution_convert_fusion.1
  10.9 0.8 fusion.35
  11.6 0.7 scatter_fusion
  12.4 0.7 scatter_fusion.2
  13.1 1.5 pad_maximum_fusion.4
  14.6 0.0 all-gather.6.cloned.1.call-update
  14.7 0.0 all-gather.10.cloned.1.call-start
  14.7 0.7 all-gather.10.cloned.1.call-update
  15.4 0.0 all-gather.8.cloned.1.call-start
  15.5 1.9 convolution_convert_fusion.2
  17.4 0.7 scatter_fusion.1
  18.1 1.9 convolution_convert_fusion
  20.1 0.7 scatter_fusion.3
  20.8 1.5 pad_maximum_fusion.2
  22.3 0.0 all-gather.8.cloned.1.call-update
  22.4 0.0 all-gather.12.cloned.1.call-start
  22.4 0.5 all-gather.12.cloned.1.call-update
  22.9 0.8 slice_bitcast_fusion
  23.7 0.1 fusion.32
  23.8 0.1 fusion.33
  24.5 0.5 not_and_fusion.1
  25.1 46.2 %all-gather = bf16[32,1,256]{2,1,0:T(2,128)(2,1)S(1)} all-gather(bf16[1,1,256]{2,1,0:T(2,128)(2,1)S(1)} %reshape.208), channel_id=1, replica_groups=mesh['file'=8,'blk'=32] {'blk'}, dimensions={0}, use_global_device_ids=true | all-gather | bytes 16896 | tf_op jit(solution)/shard_map/all_gather | solution.py:81
  71.3 0.1 compare_reduce_fusion
  71.5 1.3 copy.46
  72.7 26.9 %all-gather.6.cloned.1.call-done = bf16[8192,256]{1,0:T(8,128)(2,1)} async-done(((bf16[256,256]{1,0:T(8,128)(2,1)}), bf16[8192,256]{1,0:T(8,128)(2,1)}) %all-gather.6.cloned.1.call-update) | async-done | bytes 4194320 | tf_op jit(solution)/shard_map/all_gather | solution.py:79
  99.6 6.4 %copy.45 = bf16[8192,256]{0,1:T(8,128)(2,1)} copy(bf16[8192,256]{1,0:T(8,128)(2,1)} %all-gather.6.cloned.1.call-done) | data formatting | bytes 8388608 | tf_op jit(solution)/shard_map/all_gather | solution.py:79
  106.0 24.6 %bitcast_reduce_fusion.1 = (f32[2,128,7]{1,2,0:T(8,128)S(1)}, f32[2,8192,128,7]{2,1,3,0:T(8,128)}) fusion(pred[8192]{0:T(1024)(128)(4,1)S(1)} %reshape.211, bf16[8192,2,128,1]{0,2,3,1:T(8,128)(2,1)} %bitcast.95, bf16[128,2,7,128]{0,3,2,1:T(8,128)(2,1)S(1)} %bitcast.99), kind=kOutput, calls=%fused_computation.8 | convolution fusion | flops 3802134784 | bytes 63388672 | tf_op jit(solution)/shard_map/sgrd,kgd->gsrk/dot_general | solution.py:18
  130.6 50.8 %all-gather.10.cloned.1.call-done = bf16[8192,256]{1,0:T(8,128)(2,1)} async-done(((bf16[256,256]{1,0:T(8,128)(2,1)}), bf16[8192,256]{1,0:T(8,128)(2,1)}) %all-gather.10.cloned.1.call-update) | async-done | bytes 4194320 | tf_op jit(solution)/shard_map/all_gather | solution.py:79
  181.3 6.4 %copy.52 = bf16[8192,256]{0,1:T(8,128)(2,1)} copy(bf16[8192,256]{1,0:T(8,128)(2,1)} %all-gather.10.cloned.1.call-done) | data formatting | bytes 8388608 | tf_op jit(solution)/shard_map/all_gather | solution.py:79
  187.7 49.4 %fusion.2 = (f32[2,128,7]{1,2,0:T(8,128)S(1)}, f32[2,128,7]{1,2,0:T(8,128)S(1)}, f32[2,8192,128,7]{2,1,3,0:T(8,128)}) fusion(f32[2,8192,128,7]{2,1,3,0:T(8,128)} %get-tuple-element.18, f32[2,128,7]{1,2,0:T(8,128)S(1)} %broadcast_maximum_fusion.1, pred[8192]{0:T(1024)(128)(4,1)S(1)} %reshape.211, bf16[8192,2,128,1]{0,2,3,1:T(8,128)(2,1)} %bitcast.96, ...), kind=kOutput, calls=%fused_computation.12 | convolution fusion | flops 3860853248 | bytes 122123264 | tf_op jit(solution)/shard_map/sgrd,kgd->gsrk/dot_general | solution.py:18
  237.1 26.0 %all-gather.8.cloned.1.call-done = bf16[8192,256]{1,0:T(8,128)(2,1)} async-done(((bf16[256,256]{1,0:T(8,128)(2,1)}), bf16[8192,256]{1,0:T(8,128)(2,1)}) %all-gather.8.cloned.1.call-update) | async-done | bytes 4194320 | tf_op jit(solution)/shard_map/all_gather | solution.py:80
  263.0 6.4 %copy.49 = bf16[8192,256]{0,1:T(8,128)(2,1)} copy(bf16[8192,256]{1,0:T(8,128)(2,1)} %all-gather.8.cloned.1.call-done) | data formatting | bytes 8388608 | tf_op jit(solution)/shard_map/all_gather | solution.py:80
  269.4 22.8 %fusion.21 = bf16[128,2,7,128]{0,3,2,1:T(8,128)(2,1)S(1)} fusion(bf16[8192,2,128,1]{0,2,3,1:T(8,128)(2,1)} %bitcast.98, f32[2,8192,128,7]{2,1,3,0:T(8,128)} %get-tuple-element.18, f32[2,128,7]{1,2,0:T(8,128)S(1)} %broadcast_maximum_fusion.1, pred[8192]{0:T(1024)(128)(4,1)S(1)} %reshape.211, f32[128,2,7]{0,2,1:T(8,128)S(1)} %bitcast.104), kind=kOutput, calls=%fused_computation.23 | convolution fusion | flops 3817275392 | bytes 63395840 | tf_op jit(solution)/shard_map/gsrk,kgd->gsrd/dot_general | solution.py:25
  292.2 0.2 copy.51
  292.5 0.0 copy-start.1
  292.5 19.4 %fusion.4 = f32[2,128,7]{1,2,0:T(8,128)S(1)} fusion(f32[2,8192,128,7]{2,1,3,0:T(8,128)} %get-tuple-element.19, f32[2,128,7]{1,2,0:T(8,128)S(1)} %broadcast_maximum_fusion, pred[8192]{0:T(1024)(128)(4,1)S(1)} %reshape.211), kind=kLoop, calls=%fused_computation.14 | loop fusion | flops 58718464 | bytes 58742784 | tf_op jit(solution)/shard_map/reduce_sum | solution.py:24
  311.9 0.0 copy-start.3
  311.9 0.0 copy-start.2
  311.9 32.7 %all-gather.12.cloned.1.call-done = bf16[8192,256]{1,0:T(8,128)(2,1)} async-done(((bf16[256,256]{1,0:T(8,128)(2,1)}), bf16[8192,256]{1,0:T(8,128)(2,1)}) %all-gather.12.cloned.1.call-update) | async-done | bytes 4194320 | tf_op jit(solution)/shard_map/all_gather | solution.py:80
  344.6 6.4 %copy.55 = bf16[8192,256]{0,1:T(8,128)(2,1)} copy(bf16[8192,256]{1,0:T(8,128)(2,1)} %all-gather.12.cloned.1.call-done) | data formatting | bytes 8388608 | tf_op jit(solution)/shard_map/all_gather | solution.py:80
  351.0 22.7 %fusion.18 = bf16[128,2,7,128]{0,3,2,1:T(8,128)(2,1)S(1)} fusion(bf16[8192,2,128,1]{0,2,3,1:T(8,128)(2,1)} %bitcast.97, f32[2,8192,128,7]{2,1,3,0:T(8,128)} %get-tuple-element.19, f32[2,128,7]{1,2,0:T(8,128)S(1)} %broadcast_maximum_fusion, pred[8192]{0:T(1024)(128)(4,1)S(1)} %reshape.211, f32[128,2,7]{0,2,1:T(8,128)S(1)} %bitcast.103), kind=kOutput, calls=%fused_computation.22 | convolution fusion | flops 3817275392 | bytes 63395840 | tf_op jit(solution)/shard_map/gsrk,kgd->gsrd/dot_general | solution.py:25
  373.7 0.2 copy.57
  373.9 0.0 copy-done.3
  373.9 0.1 select_convert_fusion.1
  374.1 0.0 copy-done.2
  374.1 0.1 select_convert_fusion
  374.2 1.0 pad_maximum_fusion
  375.2 0.0 copy-done.1
  (7 shorter events, 0.1 us)
Async XLA Ops:
  6.5 1.8 copy-start
  6.5 93.1 %all-gather.6.cloned.1.call-start = ((), (), s32[]{:S(2)}) async-start(), calls=%async_computation | async-start | bytes 4325376 | tf_op jit(solution)/shard_map/all_gather | solution.py:79
  14.7 166.7 %all-gather.10.cloned.1.call-start = ((), (), s32[]{:S(2)}) async-start(), calls=%async_computation.2 | async-start | bytes 4325376 | tf_op jit(solution)/shard_map/all_gather | solution.py:79
  15.4 247.6 %all-gather.8.cloned.1.call-start = ((), (), s32[]{:S(2)}) async-start(), calls=%async_computation.1 | async-start | bytes 4325376 | tf_op jit(solution)/shard_map/all_gather | solution.py:80
  22.4 322.3 %all-gather.12.cloned.1.call-start = ((), (), s32[]{:S(2)}) async-start(), calls=%async_computation.3 | async-start | bytes 4325376 | tf_op jit(solution)/shard_map/all_gather | solution.py:80
  292.5 82.8 %copy-start.1 = (bf16[3584,256]{1,0:T(8,128)(2,1)S(1)}, bf16[3584,256]{1,0:T(8,128)(2,1)}, u32[]{:S(2)}) copy-start(bf16[3584,256]{1,0:T(8,128)(2,1)} %param.18) | copy-start | bytes 5505028
  311.9 62.0 %copy-start.3 = (pred[128]{0:T(512)(128)(4,1)S(1)}, pred[128]{0:T(512)(128)(4,1)}, u32[]{:S(2)}) copy-start(pred[128]{0:T(512)(128)(4,1)} %get-tuple-element.15) | copy-start | bytes 388
  311.9 62.2 %copy-start.2 = (pred[128]{0:T(512)(128)(4,1)S(1)}, pred[128]{0:T(512)(128)(4,1)}, u32[]{:S(2)}) copy-start(pred[128]{0:T(512)(128)(4,1)} %get-tuple-element.16) | copy-start | bytes 388
Sparse Core Ops, SparseCore 0:
  14.8 84.7 all-gather.5
  102.2 79.0 all-gather.9
  183.9 79.0 all-gather.7
  265.5 79.0 all-gather.11
where the time goes:
time: 383 us; the launch traced here: 382 us
  waiting for transfers between devices  138 us (36%)
  matrix products  126 us (33%)
  blocking collectives  46.2 us (12%)
  local copies, waits for them, and re-layouts  32.7 us (9%)
  other arithmetic  25.4 us (7%)
  between operations  13.9 us (4%)
    all_gather x2, waiting for transfers between devices, per_device(): lax.all_gather(joined_keys, 'blk', axis=0, tiled=True)  77.6 us
    dot_general x2, matrix products, attend_piece(): jnp.einsum('sgrd,kgd->gsrk', heads_of_queries, heads_of_keys, preferred_e...  73.9 us
    all_gather x2, waiting for transfers between devices, per_device(): lax.all_gather(joined_values, 'blk', axis=0, tiled=True)  58.7 us
    all_gather x1, blocking collectives, per_device(): lax.all_gather(joined_flags, 'blk', axis=0, tiled=True) > 0.5  46.2 us
    dot_general x2, matrix products, attend_piece(): jnp.einsum('gsrk,kgd->gsrd', expw.astype(jnp.bfloat16), heads_of_values,...  45.5 us
    reduce_sum x1, other arithmetic, attend_piece(): row_sum = jnp.sum(expw, axis=-1)  19.4 us
    all_gather x2, local copies, waits for them, and re-layouts, per_device(): lax.all_gather(joined_keys, 'blk', axis=0, tiled=True)  12.7 us
    all_gather x2, local copies, waits for them, and re-layouts, per_device(): lax.all_gather(joined_values, 'blk', axis=0, tiled=True)  12.7 us
  transfers between devices with their start and end apart: 4, of which 4 were waited for; matrix products, arithmetic and copies ran while one was open for 38% of the time, Pallas kernels for 0%

commit v1 on v0

--- a/solution.py
+++ b/solution.py
@@ -77,7 +77,10 @@
             starting,
             heads_of_queries,
             lax.all_gather(joined_keys, "blk", axis=0, tiled=True),
-            lax.all_gather(joined_values, "blk", axis=0, tiled=True),
+            jnp.concatenate(
+                lax.all_to_all(jnp.stack([joined_values] * lax.axis_size("blk")), "blk", 0, 0),
+                axis=0,
+            ),
             lax.all_gather(joined_flags, "blk", axis=0, tiled=True) > 0.5,
         )
         attention_output = (

time: 383 us -> 433 us (1.13); the launches traced: 382 us -> 427 us
  blocking collectives: 46.2 us -> 148 us
  waiting for transfers between devices: 138 us -> 44 us
  local copies, waits for them, and re-layouts: 32.7 us -> 52.9 us
  starting transfers between devices: 0.12 us -> 17.6 us
    all_gather x1, blocking collectives: 46.2 us -> 148 us  [per_device(): lax.all_gather(joined_flags, 'blk', axis=0, tiled=True) > 0.5]
    all_gather x2 -> x0, waiting for transfers between devices: 58.7 us -> none  [per_device(): lax.all_gather(joined_values, 'blk', axis=0, tiled=True)]
    all_gather x2, waiting for transfers between devices: 77.6 us -> 43.2 us  [per_device(): lax.all_gather(joined_keys, 'blk', axis=0, tiled=True)]
    another operation x0 -> x4, local copies, waits for them, and re-layouts: none -> 19.7 us  [the longest x2 14.8 us: attend_piece(): value_matrix.reshape(row_count, KEY_VALUE_HEADS, HEAD_WIDTH)]
    all_to_all x0 -> x2, starting transfers between devices: none -> 17.6 us  [per_device(): lax.all_to_all(jnp.stack([joined_values] * lax.axis_size('blk')), 'blk',...]
    all_to_all x0 -> x2, local copies, waits for them, and re-layouts: none -> 13 us  [per_device(): lax.all_to_all(jnp.stack([joined_values] * lax.axis_size('blk')), 'blk',...]
    all_gather x2 -> x0, local copies, waits for them, and re-layouts: 12.7 us -> none  [per_device(): lax.all_gather(joined_values, 'blk', axis=0, tiled=True)]
  transfers between devices with their start and end apart: 4 -> 4, of which waited for: 4 -> 1; matrix products, arithmetic and copies ran while one was open for 38% -> 32% of each run, Pallas kernels for 0% -> 0%
where the time goes in v1:
time: 433 us; the launch traced here: 427 us
  blocking collectives  148 us (34%)
  matrix products  126 us (29%)
  local copies, waits for them, and re-layouts  52.9 us (12%)
  waiting for transfers between devices  44 us (10%)
  other arithmetic  24.6 us (6%)
  starting transfers between devices  17.6 us (4%)
  between operations  14.3 us (3%)
    all_gather x1, blocking collectives, per_device(): lax.all_gather(joined_flags, 'blk', axis=0, tiled=True) > 0.5  148 us
    dot_general x2, matrix products, attend_piece(): jnp.einsum('sgrd,kgd->gsrk', heads_of_queries, heads_of_keys, preferred_e...  74.1 us
    dot_general x2, matrix products, attend_piece(): jnp.einsum('gsrk,kgd->gsrd', expw.astype(jnp.bfloat16), heads_of_values,...  45.3 us
    all_gather x2, waiting for transfers between devices, per_device(): lax.all_gather(joined_keys, 'blk', axis=0, tiled=True)  43.2 us
    reduce_sum x1, other arithmetic, attend_piece(): row_sum = jnp.sum(expw, axis=-1)  19.2 us
    all_to_all x2, starting transfers between devices, per_device(): lax.all_to_all(jnp.stack([joined_values] * lax.axis_size('blk')), 'blk',...  17.6 us
    another operation x2, local copies, waits for them, and re-layouts, attend_piece(): value_matrix.reshape(row_count, KEY_VALUE_HEADS, HEAD_WIDTH)  14.8 us
    all_to_all x2, local copies, waits for them, and re-layouts, per_device(): lax.all_to_all(jnp.stack([joined_values] * lax.axis_size('blk')), 'blk',...  13 us
  transfers between devices with their start and end apart: 4, of which 1 were waited for; matrix products, arithmetic and copies ran while one was open for 32% of the time, Pallas kernels for 0%

profile of v1, /device:TPU:2, one launch (start us, length us, event | category | flops | bytes accessed | tf_op | source)
XLA Modules:
  0.0 426.9 jit_solution(11732396096783201669)
XLA Ops:
  6.5 0.0 copy-start
  6.5 0.0 all-gather.4.cloned.1.call-start
  6.5 1.0 copy.81
  7.5 0.8 copy.82
  8.4 0.0 copy-done
  8.4 1.2 convolution_convert_fusion.3
  9.6 1.3 convolution_convert_fusion.1
  10.9 0.8 fusion.45
  11.6 0.7 scatter_fusion
  12.4 0.7 scatter_fusion.2
  13.1 1.5 pad_maximum_fusion.4
  14.6 0.0 all-gather.4.cloned.1.call-update
  14.7 1.9 convolution_convert_fusion.2
  16.6 0.7 scatter_fusion.1
  17.3 1.9 convolution_convert_fusion
  19.3 0.7 scatter_fusion.3
  20.0 0.9 pad_maximum_fusion.2
  20.9 0.1 copy.51
  21.0 2.4 stack.6
  23.4 11.6 %all-to-all-start = ((bf16[32,256,256]{1,2,0:T(8,128)(2,1)}), bf16[32,256,256]{1,2,0:T(8,128)(2,1)}, u32[]{:S(2)}, u32[]{:S(2)}) async-start(bf16[32,256,256]{1,2,0:T(8,128)(2,1)} %stack.6), calls=%async_computation | async-start | bytes 8388608 | tf_op jit(solution)/shard_map/all_to_all | solution.py:81
  35.0 0.0 all-gather.6.cloned.1.call-start
  35.1 0.7 all-gather.6.cloned.1.call-update
  36.4 0.8 slice_bitcast_fusion
  37.2 0.1 fusion.42
  37.3 0.1 fusion.43
  37.4 0.6 not_and_fusion.1
  38.0 147.8 %all-gather = bf16[32,1,256]{2,1,0:T(2,128)(2,1)S(1)} all-gather(bf16[1,1,256]{2,1,0:T(2,128)(2,1)S(1)} %reshape.204), channel_id=1, replica_groups=mesh['file'=8,'blk'=32] {'blk'}, dimensions={0}, use_global_device_ids=true | all-gather | bytes 16896 | tf_op jit(solution)/shard_map/all_gather | solution.py:84
  185.7 0.1 compare_reduce_fusion
  185.9 1.3 copy.48
  187.1 0.1 copy.58
  187.2 0.0 all-to-all-done
  187.3 2.5 stack.7
  189.8 6.0 %all-to-all-start.1 = ((bf16[32,256,256]{1,2,0:T(8,128)(2,1)}), bf16[32,256,256]{1,2,0:T(8,128)(2,1)}, u32[]{:S(2)}, u32[]{:S(2)}) async-start(bf16[32,256,256]{1,2,0:T(8,128)(2,1)} %stack.7), calls=%async_computation.1 | async-start | bytes 8388608 | tf_op jit(solution)/shard_map/all_to_all | solution.py:81
  195.8 6.5 %copy.52 = bf16[32,256,256]{1,0,2:T(8,128)(2,1)} copy(bf16[32,256,256]{1,2,0:T(8,128)(2,1)} %all-to-all-done) | data formatting | bytes 8388608 | tf_op jit(solution)/shard_map/all_to_all | solution.py:81
  202.3 7.4 %reshape.209 = bf16[8192,2,128,1]{0,2,1,3:T(8,128)(2,1)} reshape(bf16[32,256,256]{1,0,2:T(8,128)(2,1)} %copy.52) | data formatting | bytes 8388608 | tf_op jit(solution)/shard_map/reshape;reshape | solution.py:17
  209.7 0.0 all-gather.4.cloned.1.call-done
  209.7 6.3 %copy.47 = bf16[8192,256]{0,1:T(8,128)(2,1)} copy(bf16[8192,256]{1,0:T(8,128)(2,1)} %all-gather.4.cloned.1.call-done) | data formatting | bytes 8388608 | tf_op jit(solution)/shard_map/all_gather | solution.py:79
  216.0 24.8 %bitcast_reduce_fusion.1 = (f32[2,128,7]{1,2,0:T(8,128)S(1)}, f32[2,8192,128,7]{2,1,3,0:T(8,128)}) fusion(pred[8192]{0:T(1024)(128)(4,1)S(1)} %reshape.207, bf16[8192,2,128,1]{0,2,3,1:T(8,128)(2,1)} %bitcast.101, bf16[128,2,7,128]{0,3,2,1:T(8,128)(2,1)S(1)} %bitcast.103), kind=kOutput, calls=%fused_computation.8 | convolution fusion | flops 3802134784 | bytes 63388672 | tf_op jit(solution)/shard_map/sgrd,kgd->gsrk/dot_general | solution.py:18
  240.8 43.2 %all-gather.6.cloned.1.call-done = bf16[8192,256]{1,0:T(8,128)(2,1)} async-done(((bf16[256,256]{1,0:T(8,128)(2,1)}), bf16[8192,256]{1,0:T(8,128)(2,1)}) %all-gather.6.cloned.1.call-update) | async-done | bytes 4194320 | tf_op jit(solution)/shard_map/all_gather | solution.py:79
  284.1 6.4 %copy.55 = bf16[8192,256]{0,1:T(8,128)(2,1)} copy(bf16[8192,256]{1,0:T(8,128)(2,1)} %all-gather.6.cloned.1.call-done) | data formatting | bytes 8388608 | tf_op jit(solution)/shard_map/all_gather | solution.py:79
  290.5 49.3 %fusion.2 = (f32[2,128,7]{1,2,0:T(8,128)S(1)}, f32[2,128,7]{1,2,0:T(8,128)S(1)}, f32[2,8192,128,7]{2,1,3,0:T(8,128)}) fusion(f32[2,8192,128,7]{2,1,3,0:T(8,128)} %get-tuple-element.18, f32[2,128,7]{1,2,0:T(8,128)S(1)} %broadcast_maximum_fusion.1, pred[8192]{0:T(1024)(128)(4,1)S(1)} %reshape.207, bf16[8192,2,128,1]{0,2,3,1:T(8,128)(2,1)} %bitcast.102, ...), kind=kOutput, calls=%fused_computation.12 | convolution fusion | flops 3860853248 | bytes 122123264 | tf_op jit(solution)/shard_map/sgrd,kgd->gsrk/dot_general | solution.py:18
  339.8 22.6 %fusion.29 = bf16[128,2,7,128]{0,3,2,1:T(8,128)(2,1)S(1)} fusion(f32[2,8192,128,7]{2,1,3,0:T(8,128)} %get-tuple-element.18, f32[2,128,7]{1,2,0:T(8,128)S(1)} %broadcast_maximum_fusion.1, pred[8192]{0:T(1024)(128)(4,1)S(1)} %reshape.207, bf16[8192,2,128,1]{0,2,1,3:T(8,128)(2,1)} %reshape.209, f32[128,2,7]{0,2,1:T(8,128)S(1)} %bitcast.108), kind=kOutput, calls=%fused_computation.25 | convolution fusion | flops 3817275392 | bytes 63395840 | tf_op jit(solution)/shard_map/gsrk,kgd->gsrd/dot_general | solution.py:25
  362.4 0.2 copy.54
  362.6 0.0 all-to-all-done.1
  362.6 6.5 %copy.59 = bf16[32,256,256]{1,0,2:T(8,128)(2,1)} copy(bf16[32,256,256]{1,2,0:T(8,128)(2,1)} %all-to-all-done.1) | data formatting | bytes 8388608 | tf_op jit(solution)/shard_map/all_to_all | solution.py:81
  369.1 7.4 %reshape.211 = bf16[8192,2,128,1]{0,2,1,3:T(8,128)(2,1)} reshape(bf16[32,256,256]{1,0,2:T(8,128)(2,1)} %copy.59) | data formatting | bytes 8388608 | tf_op jit(solution)/shard_map/reshape;reshape | solution.py:17
  376.5 19.2 %fusion.4 = f32[2,128,7]{1,2,0:T(8,128)S(1)} fusion(f32[2,8192,128,7]{2,1,3,0:T(8,128)} %get-tuple-element.19, f32[2,128,7]{1,2,0:T(8,128)S(1)} %broadcast_maximum_fusion, pred[8192]{0:T(1024)(128)(4,1)S(1)} %reshape.207), kind=kLoop, calls=%fused_computation.14 | loop fusion | flops 58718464 | bytes 58742784 | tf_op jit(solution)/shard_map/reduce_sum | solution.py:24
  395.7 0.0 copy-start.1
  395.7 0.0 copy-start.3
  395.7 0.0 copy-start.2
  395.7 22.8 %fusion.24 = bf16[128,2,7,128]{0,3,2,1:T(8,128)(2,1)S(1)} fusion(f32[2,8192,128,7]{2,1,3,0:T(8,128)} %get-tuple-element.19, f32[2,128,7]{1,2,0:T(8,128)S(1)} %broadcast_maximum_fusion, pred[8192]{0:T(1024)(128)(4,1)S(1)} %reshape.207, bf16[8192,2,128,1]{0,2,1,3:T(8,128)(2,1)} %reshape.211, f32[128,2,7]{0,2,1:T(8,128)S(1)} %bitcast.107), kind=kOutput, calls=%fused_computation.24 | convolution fusion | flops 3817275392 | bytes 63395840 | tf_op jit(solution)/shard_map/gsrk,kgd->gsrd/dot_general | solution.py:25
  418.5 0.2 copy.61
  418.7 0.0 copy-done.3
  418.7 0.1 select_convert_fusion.1
  418.9 0.0 copy-done.2
  418.9 0.1 select_convert_fusion
  419.0 1.0 pad_maximum_fusion
  420.0 0.0 copy-done.1
  (7 shorter events, 0.1 us)
Async XLA Ops:
  6.5 1.8 copy-start
  6.5 203.1 %all-gather.4.cloned.1.call-start = ((), (), s32[]{:S(2)}) async-start(), calls=%async_computation.2 | async-start | bytes 4325376 | tf_op jit(solution)/shard_map/all_gather | solution.py:79
  23.4 163.9 %all-to-all-start = ((bf16[32,256,256]{1,2,0:T(8,128)(2,1)}), bf16[32,256,256]{1,2,0:T(8,128)(2,1)}, u32[]{:S(2)}, u32[]{:S(2)}) async-start(bf16[32,256,256]{1,2,0:T(8,128)(2,1)} %stack.6), calls=%async_computation | async-start | bytes 8388608 | tf_op jit(solution)/shard_map/all_to_all | solution.py:81
  35.0 249.1 %all-gather.6.cloned.1.call-start = ((), (), s32[]{:S(2)}) async-start(), calls=%async_computation.3 | async-start | bytes 4325376 | tf_op jit(solution)/shard_map/all_gather | solution.py:79
  189.8 172.9 %all-to-all-start.1 = ((bf16[32,256,256]{1,2,0:T(8,128)(2,1)}), bf16[32,256,256]{1,2,0:T(8,128)(2,1)}, u32[]{:S(2)}, u32[]{:S(2)}) async-start(bf16[32,256,256]{1,2,0:T(8,128)(2,1)} %stack.7), calls=%async_computation.1 | async-start | bytes 8388608 | tf_op jit(solution)/shard_map/all_to_all | solution.py:81
  395.7 24.3 %copy-start.1 = (bf16[3584,256]{1,0:T(8,128)(2,1)S(1)}, bf16[3584,256]{1,0:T(8,128)(2,1)}, u32[]{:S(2)}) copy-start(bf16[3584,256]{1,0:T(8,128)(2,1)} %param.18) | copy-start | bytes 5505028
  395.7 23.0 %copy-start.3 = (pred[128]{0:T(512)(128)(4,1)S(1)}, pred[128]{0:T(512)(128)(4,1)}, u32[]{:S(2)}) copy-start(pred[128]{0:T(512)(128)(4,1)} %get-tuple-element.15) | copy-start | bytes 388
  395.7 23.2 %copy-start.2 = (pred[128]{0:T(512)(128)(4,1)S(1)}, pred[128]{0:T(512)(128)(4,1)}, u32[]{:S(2)}) copy-start(pred[128]{0:T(512)(128)(4,1)} %get-tuple-element.16) | copy-start | bytes 388
Sparse Core Ops, SparseCore 0:
  14.8 130.4 all-gather.3
  147.9 136.1 all-gather.5
